TPU v7x, 32 devices: a whole 2x2x4 slice. The times are simulated.
32 devices in a mesh: dp: 8 (over z, x), row: 2 (over y), col: 2 (over core).
Axes of the slice: x: 2, y: 2, z: 4, core: 2. Of those that a mesh axis runs over, the one named last changes fastest.
Arguments:
- block_input: float32 [4096, 640], P(('dp', 'col'), 'row'), may hold values from -200 to 200
- segment_ids: int32 [16, 256], P(('dp', 'row')), may hold values from 0 to 3, never falling along the last dimension, each value on 1 to 128 neighbouring positions
- w_query: bfloat16 [640, 1024], P('row', 'col'), may hold values from -0.25 to 0.25
- w_key: bfloat16 [640, 256], P('row'), may hold values from -0.25 to 0.25
- w_value: bfloat16 [640, 256], P('row'), may hold values from -0.25 to 0.25
- w_out: bfloat16 [1024, 640], P('col', 'row'), may hold values from -0.1875 to 0.1875
- w_gate: bfloat16 [640, 2048], P('row', 'col'), may hold values from -0.25 to 0.25
- w_up: bfloat16 [640, 2048], P('row', 'col'), may hold values from -0.25 to 0.25
- w_down: bfloat16 [2048, 640], P('col', 'row'), may hold values from -0.125 to 0.125
- gain_input: float32 [640], P('row'), may hold values from 0.25 to 1.75
- gain_attn: float32 [640], P('row'), may hold values from 0.25 to 1.75
- gain_ffn_pre: float32 [640], P('row'), may hold values from 0.25 to 1.75
- gain_ffn_post: float32 [640], P('row'), may hold values from 0.25 to 1.75
- gain_query: float32 [256], replicated, may hold values from 0.25 to 1.75
- gain_key: float32 [256], replicated, may hold values from 0.25 to 1.75
- out_cotangent: float32 [4096, 640], P(('dp', 'col'), 'row'), may hold values from -6 to 6
Outputs:
- block_output: float32 [4096, 640], P(('dp', 'col'), 'row')
- input_grad: float32 [4096, 640], P(('dp', 'col'), 'row')
- query_grad: float32 [640, 1024], P('row', 'col')
- key_grad: float32 [640, 256], P('row')
- value_grad: float32 [640, 256], P('row')
- out_grad: float32 [1024, 640], P('col', 'row')
- gate_grad: float32 [640, 2048], P('row', 'col')
- up_grad: float32 [640, 2048], P('row', 'col')
- down_grad: float32 [2048, 640], P('col', 'row')
- gain_input_grad: float32 [640], P('row')
- gain_attn_grad: float32 [640], P('row')
- gain_ffn_pre_grad: float32 [640], P('row')
- gain_ffn_post_grad: float32 [640], P('row')
- gain_query_grad: float32 [256], replicated
- gain_key_grad: float32 [256], replicated
Inputs may be any that keep to these rules, and one draw needn't show every extreme that they name: `segment_ids`: one packed sequence a row; document numbers never fall, start at 0 and take every value up to 3; each document has 1 to 128 tokens and one has exactly 128.
All inputs are finite; a program needn't handle non-finite values.
Results may differ from a plain program's by a relative error of at most 0.014.
Values may be sent and summed in bfloat16 or wider, within the bound.
No kernel may reach another device: no remote copies, remote signals or barrier semaphores. Data moves between devices by JAX's collectives and lax.ppermute only.
A program may use at most 64 MiB of HBM per device.

v0:
```python
import jax
import jax.numpy as jnp
from jax import lax
from jax.sharding import PartitionSpec as P

D = 640
HD = 256
eps_norm = 1e-06
rope_base = 1000000.0


def rms_scale(values):
    return lax.rsqrt(jnp.mean(values * values, axis=-1, keepdims=True) + eps_norm)


def rope_tables(segments):
    length = segments.shape[-1]
    places = jnp.arange(length, dtype=jnp.int32)
    earlier = jnp.concatenate([segments[..., :1] - 1, segments[..., :-1]], axis=-1)
    starts = lax.cummax(jnp.where(segments != earlier, places, 0), axis=segments.ndim - 1)
    offsets = (places - starts).astype(jnp.float32)
    frequency = rope_base ** (-(jnp.arange(HD // 2, dtype=jnp.float32) * 2.0 / HD))
    angles = offsets[..., None] * frequency
    return (jnp.cos(angles), jnp.sin(angles))


def rotate(values, cosine_table, sine_table):
    lower_half = values[..., : HD // 2]
    upper_half = values[..., HD // 2 :]
    return jnp.concatenate(
        [
            lower_half * cosine_table - upper_half * sine_table,
            upper_half * cosine_table + lower_half * sine_table,
        ],
        axis=-1,
    )


def gelu_tanh(values):
    return jax.nn.gelu(values, approximate=True)


def width_total(values):
    return lax.psum(values, "row")


def norm_forward(values, gain_vector):
    squares = width_total(jnp.sum(values * values, axis=1, keepdims=True))
    inv_rms = lax.rsqrt(squares / D + eps_norm)
    return (values * inv_rms * gain_vector, inv_rms)


def norm_backward(upstream, values, inv_rms, gain_vector):
    weighted = upstream * gain_vector
    width_sum = width_total(jnp.sum(weighted * values, axis=1, keepdims=True))
    through = inv_rms * weighted - values * inv_rms**3 * width_sum / D
    return (through, jnp.sum(upstream * values * inv_rms, axis=0))


def token_gather(values):
    return lax.all_gather(values, "col", axis=0, tiled=True)


def hidden_gather(values):
    return lax.all_gather(values, "row", axis=0, tiled=True)


def rows_term(gathered, weight, contract):
    return lax.dot_general(
        gathered, weight, (((1,), (contract,)), ((), ())), preferred_element_type=jnp.float32
    )


def project_sum(gathered, weight, contract):
    return lax.psum_scatter(
        rows_term(gathered, weight, contract), "row", scatter_dimension=0, tiled=True
    )


def column_sum(gathered, weight, contract):
    return lax.psum_scatter(
        rows_term(gathered, weight, contract), "col", scatter_dimension=0, tiled=True
    )


def weight_term(left, right):
    return lax.dot_general(
        left, right, (((0,), (0,)), ((), ())), preferred_element_type=jnp.float32
    )


def attention_forward(query_bf, key_bf, value_bf, allowed, logit_scale_factor):
    seq_rows, head_count = (query_bf.shape[0], query_bf.shape[1])
    block_rows = min(512, seq_rows)
    block_count = seq_rows // block_rows
    query_blocks = query_bf.reshape(block_count, block_rows, head_count, HD)
    mask_blocks = allowed.reshape(block_count, block_rows, seq_rows)

    def one_block(operands):
        query_part, mask_part = operands
        attention_logits = (
            jnp.einsum("qhd,kd->hqk", query_part, key_bf, preferred_element_type=jnp.float32)
            * logit_scale_factor
        )
        weights = jnp.where(mask_part[None], jnp.exp(attention_logits), 0.0)
        row_total = jnp.sum(weights, axis=2, keepdims=True)
        probabilities = (weights / row_total).astype(jnp.bfloat16)
        mixed_head_outputs = jnp.einsum(
            "hqk,kd->qhd", probabilities, value_bf, preferred_element_type=jnp.float32
        )
        return (mixed_head_outputs, jnp.log(row_total))

    mixed_head_outputs, log_total = lax.map(one_block, (query_blocks, mask_blocks))
    return (mixed_head_outputs.reshape(seq_rows, head_count * HD), log_total)


def attention_backward(
    query_bf, key_bf, value_bf, allowed, logit_scale_factor, log_total, grad_heads_bf
):
    seq_rows, head_count = (query_bf.shape[0], query_bf.shape[1])
    block_rows = min(512, seq_rows)
    block_count = seq_rows // block_rows
    query_blocks = query_bf.reshape(block_count, block_rows, head_count, HD)
    grad_blocks = grad_heads_bf.reshape(block_count, block_rows, head_count, HD)
    mask_blocks = allowed.reshape(block_count, block_rows, seq_rows)

    def one_block(running, operands):
        key_acc, value_acc = running
        query_part, mask_part, lse_part, grad_part = operands
        attention_logits = (
            jnp.einsum("qhd,kd->hqk", query_part, key_bf, preferred_element_type=jnp.float32)
            * logit_scale_factor
        )
        probabilities = jnp.where(mask_part[None], jnp.exp(attention_logits - lse_part), 0.0)
        prob_bf = probabilities.astype(jnp.bfloat16)
        value_acc = value_acc + jnp.einsum(
            "hqk,qhd->kd", prob_bf, grad_part, preferred_element_type=jnp.float32
        )
        probability_gradient = jnp.einsum(
            "qhd,kd->hqk", grad_part, value_bf, preferred_element_type=jnp.float32
        )
        row_delta = jnp.sum(probabilities * probability_gradient, axis=2, keepdims=True)
        score_gradient = (probabilities * (probability_gradient - row_delta)).astype(jnp.bfloat16)
        grad_query = (
            jnp.einsum("hqk,kd->qhd", score_gradient, key_bf, preferred_element_type=jnp.float32)
            * logit_scale_factor
        )
        key_acc = (
            key_acc
            + jnp.einsum(
                "hqk,qhd->kd", score_gradient, query_part, preferred_element_type=jnp.float32
            )
            * logit_scale_factor
        )
        return ((key_acc, value_acc), grad_query)

    zero_rows = jnp.zeros((seq_rows, HD), jnp.float32)
    (grad_key, grad_value), grad_query = lax.scan(
        one_block, (zero_rows, zero_rows), (query_blocks, mask_blocks, log_total, grad_blocks)
    )
    return (grad_query.reshape(seq_rows, head_count, HD), grad_key, grad_value)


def on_device(
    block_input,
    segment_ids,
    w_query,
    w_key,
    w_value,
    w_out,
    w_gate,
    w_up,
    w_down,
    gain_input,
    gain_attn,
    gain_ffn_pre,
    gain_ffn_post,
    gain_query,
    gain_key,
    out_cotangent,
):
    seq_rows = block_input.shape[0]
    query_width = w_query.shape[1]
    head_count = query_width // HD
    hidden_width = w_gate.shape[1]
    logit_scale_factor = HD ** (-0.5)
    segments = segment_ids[0]
    cosine_table, sine_table = rope_tables(segments)
    places = jnp.arange(seq_rows, dtype=jnp.int32)
    allowed = (segments[:, None] == segments[None, :]) & (places[:, None] >= places[None, :])

    def query_map(unnormed, gain_vector):
        return rotate(
            unnormed * rms_scale(unnormed) * gain_vector,
            cosine_table[:, None, :],
            sine_table[:, None, :],
        )

    def key_map(unnormed, gain_vector):
        return rotate(unnormed * rms_scale(unnormed) * gain_vector, cosine_table, sine_table)

    normed_in, scale_in = norm_forward(block_input, gain_input)
    input_all = token_gather(normed_in.astype(jnp.bfloat16))
    joint_weight = jnp.concatenate([w_query, w_key, w_value], axis=1)
    projected = project_sum(input_all, joint_weight, 0)
    raw_query = projected[:, :query_width].reshape(seq_rows, head_count, HD)
    raw_key = projected[:, query_width : query_width + HD]
    raw_value = projected[:, query_width + HD :]
    query_bf = query_map(raw_query, gain_query).astype(jnp.bfloat16)
    key_bf = key_map(raw_key, gain_key).astype(jnp.bfloat16)
    value_bf = raw_value.astype(jnp.bfloat16)
    mixed_head_outputs, log_total = attention_forward(
        query_bf, key_bf, value_bf, allowed, logit_scale_factor
    )
    heads_all = lax.all_gather(mixed_head_outputs.astype(jnp.bfloat16), "row", axis=0, tiled=True)
    attn_proj = column_sum(heads_all, w_out, 0)
    attn_normed, scale_y = norm_forward(attn_proj, gain_attn)
    resid_mid = block_input + attn_normed
    ffn_normed, scale_mid = norm_forward(resid_mid, gain_ffn_pre)
    ffn_all = token_gather(ffn_normed.astype(jnp.bfloat16))
    mix_weight = jnp.concatenate([w_gate, w_up], axis=1)
    gate_up = lax.psum_scatter(
        rows_term(ffn_all, mix_weight, 0), "row", scatter_dimension=0, tiled=True
    )
    gate_value = gate_up[:, :hidden_width]
    up_value = gate_up[:, hidden_width:]
    gelu_value, gelu_pull = jax.vjp(gelu_tanh, gate_value)
    hidden_all = hidden_gather((gelu_value * up_value).astype(jnp.bfloat16))
    ffn_out = column_sum(hidden_all, w_down, 0)
    ffn_normed_out, scale_f = norm_forward(ffn_out, gain_ffn_post)
    block_output = resid_mid + ffn_normed_out
    grad_ffn, post_part = norm_backward(out_cotangent, ffn_out, scale_f, gain_ffn_post)
    grad_ffn_all = token_gather(grad_ffn.astype(jnp.bfloat16))
    grad_hidden = project_sum(grad_ffn_all, w_down, 1)
    down_grad = weight_term(hidden_all, grad_ffn_all)
    grad_gate = gelu_pull(grad_hidden * up_value)[0]
    grad_up = grad_hidden * gelu_value
    grad_mix = jnp.concatenate([grad_gate, grad_up], axis=1).astype(jnp.bfloat16)
    grad_mix_all = lax.all_gather(grad_mix, "row", axis=0, tiled=True)
    grad_pre = column_sum(grad_mix_all, mix_weight, 1)
    mix_grad = weight_term(ffn_all, grad_mix_all)
    grad_mid_norm, pre_part = norm_backward(grad_pre, resid_mid, scale_mid, gain_ffn_pre)
    grad_mid = out_cotangent + grad_mid_norm
    grad_attn, attn_part = norm_backward(grad_mid, attn_proj, scale_y, gain_attn)
    grad_attn_all = token_gather(grad_attn.astype(jnp.bfloat16))
    grad_heads = lax.psum_scatter(
        rows_term(grad_attn_all, w_out, 1), "row", scatter_dimension=0, tiled=True
    )
    out_grad = weight_term(heads_all, grad_attn_all)
    grad_heads_bf = grad_heads.astype(jnp.bfloat16).reshape(seq_rows, head_count, HD)
    rotated_query_gradient, grad_key_rot, grad_value = attention_backward(
        query_bf, key_bf, value_bf, allowed, logit_scale_factor, log_total, grad_heads_bf
    )
    query_pull = jax.vjp(query_map, raw_query, gain_query)[1]
    grad_raw_query, query_gain_part = query_pull(rotated_query_gradient)
    key_pull = jax.vjp(key_map, raw_key, gain_key)[1]
    grad_raw_key, key_gain_part = key_pull(grad_key_rot)
    grad_joint = jnp.concatenate(
        [grad_raw_query.reshape(seq_rows, query_width), grad_raw_key, grad_value], axis=1
    ).astype(jnp.bfloat16)
    grad_joint_all = hidden_gather(grad_joint)
    grad_in = column_sum(grad_joint_all, joint_weight, 1)
    joint_grad = weight_term(input_all, grad_joint_all)
    grad_x_norm, input_part = norm_backward(grad_in, block_input, scale_in, gain_input)
    input_grad = grad_mid + grad_x_norm
    query_part_grad = joint_grad[:, :query_width]
    key_part_grad = joint_grad[:, query_width : query_width + HD]
    value_part_grad = joint_grad[:, query_width + HD :]
    query_sum, out_sum_grad, mix_sum, down_sum = lax.psum(
        (query_part_grad, out_grad, mix_grad, down_grad), "dp"
    )
    key_sum, value_sum, input_gain_sum, attn_gain_sum, pre_gain_sum, post_gain_sum = lax.psum(
        (key_part_grad, value_part_grad, input_part, attn_part, pre_part, post_part), ("dp", "col")
    )
    query_gain_sum, key_gain_sum = lax.psum((query_gain_part, key_gain_part), ("dp", "row", "col"))
    return (
        block_output,
        input_grad,
        query_sum,
        key_sum,
        value_sum,
        out_sum_grad,
        mix_sum[:, :hidden_width],
        mix_sum[:, hidden_width:],
        down_sum,
        input_gain_sum,
        attn_gain_sum,
        pre_gain_sum,
        post_gain_sum,
        query_gain_sum,
        key_gain_sum,
    )


def solution(mesh):
    placed = (
        P(("dp", "col"), "row"),
        P(("dp", "row"), None),
        P("row", "col"),
        P("row", None),
        P("row", None),
        P("col", "row"),
        P("row", "col"),
        P("row", "col"),
        P("col", "row"),
        P("row"),
        P("row"),
        P("row"),
        P("row"),
        P(),
        P(),
        P(("dp", "col"), "row"),
    )
    return jax.shard_map(
        on_device,
        mesh=mesh,
        in_specs=placed,
        out_specs=(
            P(("dp", "col"), "row"),
            P(("dp", "col"), "row"),
            P("row", "col"),
            P("row", None),
            P("row", None),
            P("col", "row"),
            P("row", "col"),
            P("row", "col"),
            P("col", "row"),
            P("row"),
            P("row"),
            P("row"),
            P("row"),
            P(),
            P(),
        ),
        check_vma=False,
    )
```

profile of v0, /device:TPU:0, one launch (start us, length us, event | category | flops | bytes accessed | tf_op | source)
XLA Modules:
  0.0 678.4 jit_solution(7398071400886092553)
XLA Ops:
  8.4 5.9 psum.140
  25.1 31.8 %reduce-scatter.9.cloned.1.call-done = f32[256,1024]{1,0:T(8,128)} async-done(((f32[512,1024]{1,0:T(8,128)}), f32[256,1024]{1,0:T(8,128)}) %reduce-scatter.9.cloned.1.call-update) | async-done | bytes 1048592 | tf_op jit(solution)/shard_map/reduce_scatter | solution.py:75
  62.4 8.5 %all_gather.25 = bf16[512,512]{0,1:T(8,128)(2,1)S(1)} all-gather(bf16[256,512]{0,1:T(8,128)(2,1)S(1)} %bitcast.105), channel_id=1, replica_groups=mesh['dp'=8,'row'=2,'col'=2] {'row'}, dimensions={0}, use_global_device_ids=true | all-gather | bytes 786432 | tf_op jit(solution)/shard_map/all_gather | solution.py:215
  75.4 5.8 reduce-scatter.11.cloned.1.call-done
  82.2 4.9 psum.141
  88.2 4.9 psum.142
  96.1 3.2 fusion.51
  99.4 55.6 %reduce-scatter.13.cloned.1.call-done = f32[256,2048]{1,0:T(8,128)} async-done(((f32[512,2048]{1,0:T(8,128)}), f32[256,2048]{1,0:T(8,128)}) %reduce-scatter.13.cloned.1.call-update) | async-done | bytes 2097168 | tf_op jit(solution)/shard_map/reduce_scatter | solution.py:222
  155.0 2.7 multiply_convert_fusion.1
  157.8 21.4 %all-gather.4.cloned.1.call-done = bf16[512,1024]{1,0:T(8,128)(2,1)} async-done(((bf16[256,1024]{1,0:T(8,128)(2,1)}), bf16[512,1024]{1,0:T(8,128)(2,1)}) %all-gather.4.cloned.1.call-update) | async-done | bytes 1048592 | tf_op jit(solution)/shard_map/all_gather | solution.py:65
  179.2 2.6 fusion.52
  181.8 8.1 %reduce-scatter.15.cloned.1.call-done = f32[256,320]{0,1:T(8,128)} async-done(((f32[512,320]{0,1:T(8,128)}), f32[256,320]{0,1:T(8,128)}) %reduce-scatter.15.cloned.1.call-update) | async-done | bytes 327696 | tf_op jit(solution)/shard_map/reduce_scatter | solution.py:81
  191.0 4.9 psum.143
  197.7 4.9 psum.144
  207.2 2.1 fusion.53
  209.4 33.1 %reduce-scatter.17.cloned.1.call-done = f32[256,1024]{1,0:T(8,128)} async-done(((f32[512,1024]{1,0:T(8,128)}), f32[256,1024]{1,0:T(8,128)}) %reduce-scatter.17.cloned.1.call-update) | async-done | bytes 1048592 | tf_op jit(solution)/shard_map/reduce_scatter | solution.py:75
  245.7 33.2 %all-gather.6.cloned.1.call-done = bf16[512,2048]{1,0:T(8,128)(2,1)} async-done(((bf16[256,2048]{1,0:T(8,128)(2,1)}), bf16[512,2048]{1,0:T(8,128)(2,1)}) %all-gather.6.cloned.1.call-update) | async-done | bytes 2097168 | tf_op jit(solution)/shard_map/all_gather | solution.py:239
  278.9 3.3 fusion.54
  282.3 8.1 %reduce-scatter.19.cloned.1.call-done = f32[256,320]{0,1:T(8,128)} async-done(((f32[512,320]{0,1:T(8,128)}), f32[256,320]{0,1:T(8,128)}) %reduce-scatter.19.cloned.1.call-update) | async-done | bytes 327696 | tf_op jit(solution)/shard_map/reduce_scatter | solution.py:81
  292.2 4.9 psum.145
  298.9 5.0 psum.146
  306.1 2.5 fusion.55
  308.9 21.4 %reduce-scatter.21.cloned.1.call-done = f32[256,512]{1,0:T(8,128)} async-done(((f32[512,512]{1,0:T(8,128)}), f32[256,512]{1,0:T(8,128)}) %reduce-scatter.21.cloned.1.call-update) | async-done | bytes 524304 | tf_op jit(solution)/shard_map/reduce_scatter | solution.py:246
  346.0 21.4 %all-gather.8.cloned.1.call-done = bf16[512,1024]{0,1:T(8,128)(2,1)} async-done(((bf16[256,1024]{0,1:T(8,128)(2,1)}), bf16[512,1024]{0,1:T(8,128)(2,1)}) %all-gather.8.cloned.1.call-update) | async-done | bytes 1048592 | tf_op jit(solution)/shard_map/all_gather | solution.py:65
  367.4 2.6 fusion.60
  371.9 2.4 fusion.58
  377.6 44.1 %all-reduce.4 = (f32[256]{0:T(256)}, f32[256]{0:T(256)}) all-reduce(f32[256]{0:T(256)S(1)} %get-tuple-element.68, f32[256]{0:T(256)S(1)} %copy-done.62), channel_id=1, replica_groups=mesh['dp'=8,'row'=2,'col'=2] {'dp','row','col'}, use_global_device_ids=true, to_apply=%region_47.48 | all-reduce | flops 512 | bytes 4096 | tf_op jit(solution)/shard_map/psum | solution.py:275
  423.8 5.4 psum.147
  431.1 33.6 %all-reduce.5 = (f32[320]{0:T(512)}, f32[320]{0:T(512)}, f32[320]{0:T(512)}, f32[320]{0:T(512)}) all-reduce(f32[320]{0:T(512)S(1)} %get-tuple-element.76, f32[320]{0:T(512)S(1)} %copy-done.61, f32[320]{0:T(512)S(1)} %copy-done.60, f32[320]{0:T(512)S(1)} %copy-done.59), channel_id=1, replica_groups=mesh['dp'=8,'row'=2,'col'=2] {'dp','col'}, use_global_device_ids=true, to_apply=%region_39.40 | all-reduce | flops 1280 | bytes 10240 | tf_op jit(solution)/shard_map/psum | solution.py:272
  464.7 105.0 %all-reduce.13.cloned.1.call-done = (f32[320,512]{1,0:T(8,128)}, f32[512,320]{0,1:T(8,128)}, f32[320,2048]{1,0:T(8,128)}, f32[1024,320]{0,1:T(8,128)}) async-done(((f32[320,512]{1,0:T(8,128)}, f32[512,320]{0,1:T(8,128)}, f32[320,2048]{1,0:T(8,128)}, f32[1024,320]{0,1:T(8,128)}), (f32[320,512]{1,0:T(8,128)}, f32[512,320]{0,1:T(8,128)}, f32[320,2048]{1,0:T(8,128)}, ...) | async-done | bytes 5242896 | tf_op jit(solution)/shard_map/psum | solution.py:269
  569.7 3.5 fusion.48
  573.3 91.3 %all-reduce.11.cloned.1.call-done = (f32[320,256]{1,0:T(8,128)}, f32[320,256]{1,0:T(8,128)}) async-done(((f32[320,256]{1,0:T(8,128)}, f32[320,256]{1,0:T(8,128)}), (f32[320,256]{1,0:T(8,128)}, f32[320,256]{1,0:T(8,128)})) %all-reduce.11.cloned.1.call-update) | async-done | bytes 655376 | tf_op jit(solution)/shard_map/psum | solution.py:272
  (244 shorter events, 74.8 us)
Async XLA Ops:
  7.2 172.0 %copy-start = (bf16[1024,320]{0,1:T(8,128)(2,1)S(1)}, bf16[1024,320]{0,1:T(8,128)(2,1)}, u32[]{:S(2)}) copy-start(bf16[1024,320]{0,1:T(8,128)(2,1)} %param.24) | copy-start | bytes 1966084
  7.2 49.6 %reduce-scatter.9.cloned.1.call-start = ((), (), s32[]{:S(2)}) async-start(), calls=%async_computation.8 | async-start | bytes 3145728 | tf_op jit(solution)/shard_map/reduce_scatter | solution.py:75
  23.0 36.9 %copy-start.50 = (f32[256]{0:T(256)S(1)}, f32[256]{0:T(256)}, u32[]{:S(2)}) copy-start(f32[256]{0:T(256)} %param.30) | copy-start | bytes 3076
  23.0 58.1 %reduce-scatter.11.cloned.1.call-start = ((), (), s32[]{:S(2)}) async-start(), calls=%async_computation.9 | async-start | bytes 983040 | tf_op jit(solution)/shard_map/reduce_scatter | solution.py:81
  24.7 35.9 %copy-start.66 = (f32[128]{0:T(128)}, f32[128]{0:T(128)S(1)}, u32[]{:S(2)}) copy-start(f32[128]{0:T(128)S(1)} %negate_power_fusion) | copy-start | bytes 1540
  25.0 36.7 %copy-start.33 = (pred[256,256]{0,1:T(8,128)(4,1)}, pred[256,256]{0,1:T(8,128)(4,1)S(1)}, u32[]{:S(2)}) copy-start(pred[256,256]{0,1:T(8,128)(4,1)S(1)} %fusion.20) | copy-start | bytes 196612
  73.0 82.0 %reduce-scatter.13.cloned.1.call-start = ((), (), s32[]{:S(2)}) async-start(), calls=%async_computation.10 | async-start | bytes 6291456 | tf_op jit(solution)/shard_map/reduce_scatter | solution.py:222
  88.2 114.4 %copy-start.4 = (f32[256,320]{0,1:T(8,128)}, f32[256,320]{0,1:T(8,128)S(1)}, u32[]{:S(2)}) copy-start(f32[256,320]{0,1:T(8,128)S(1)} %get-tuple-element.100) | copy-start | bytes 983044
  99.3 79.8 %all-gather.4.cloned.1.call-start = ((), (), s32[]{:S(2)}) async-start(), calls=%async_computation.11 | async-start | bytes 1572864 | tf_op jit(solution)/shard_map/all_gather | solution.py:65
  157.7 38.2 %copy-start.17 = (f32[256,320]{0,1:T(8,128)S(1)}, f32[256,320]{0,1:T(8,128)}, u32[]{:S(2)}) copy-start(f32[256,320]{0,1:T(8,128)} %param.31) | copy-start | bytes 983044
  157.7 38.2 %copy-start.58 = (f32[320]{0:T(512)S(1)}, f32[320]{0:T(512)}, u32[]{:S(2)}) copy-start(f32[320]{0:T(512)} %param.28) | copy-start | bytes 3844
  157.7 32.2 %reduce-scatter.15.cloned.1.call-start = ((), (), s32[]{:S(2)}) async-start(), calls=%async_computation.12 | async-start | bytes 983040 | tf_op jit(solution)/shard_map/reduce_scatter | solution.py:81
  181.8 60.7 %reduce-scatter.17.cloned.1.call-start = ((), (), s32[]{:S(2)}) async-start(), calls=%async_computation.13 | async-start | bytes 3145728 | tf_op jit(solution)/shard_map/reduce_scatter | solution.py:75
  209.3 69.6 %all-gather.6.cloned.1.call-start = ((), (), s32[]{:S(2)}) async-start(), calls=%async_computation.14 | async-start | bytes 3145728 | tf_op jit(solution)/shard_map/all_gather | solution.py:239
  245.6 44.8 %copy-start.5 = (f32[256,320]{0,1:T(8,128)S(1)}, f32[256,320]{0,1:T(8,128)}, u32[]{:S(2)}) copy-start(f32[256,320]{0,1:T(8,128)} %copy-done.4) | copy-start | bytes 983044
  245.7 51.4 %copy-start.6 = (f32[256,320]{0,1:T(8,128)S(1)}, f32[256,320]{0,1:T(8,128)}, u32[]{:S(2)}) copy-start(f32[256,320]{0,1:T(8,128)} %reduce-scatter.11.cloned.1.call-done) | copy-start | bytes 983044
  245.7 51.4 %copy-start.18 = (f32[256,320]{0,1:T(8,128)S(1)}, f32[256,320]{0,1:T(8,128)}, u32[]{:S(2)}) copy-start(f32[256,320]{0,1:T(8,128)} %param.31) | copy-start | bytes 983044
  245.7 44.7 %reduce-scatter.19.cloned.1.call-start = ((), (), s32[]{:S(2)}) async-start(), calls=%async_computation.15 | async-start | bytes 983040 | tf_op jit(solution)/shard_map/reduce_scatter | solution.py:81
  282.2 48.1 %reduce-scatter.21.cloned.1.call-start = ((), (), s32[]{:S(2)}) async-start(), calls=%async_computation.16 | async-start | bytes 1572864 | tf_op jit(solution)/shard_map/reduce_scatter | solution.py:246
  308.6 58.8 %all-gather.8.cloned.1.call-start = ((), (), s32[]{:S(2)}) async-start(), calls=%async_computation.17 | async-start | bytes 1572864 | tf_op jit(solution)/shard_map/all_gather | solution.py:65
  346.0 76.7 %reduce-scatter.23.cloned.1.call-start = ((), (), s32[]{:S(2)}) async-start(), calls=%async_computation.18 | async-start | bytes 983040 | tf_op jit(solution)/shard_map/reduce_scatter | solution.py:81
  370.0 199.8 %all-reduce.13.cloned.1.call-start = ((), (), s32[]{:S(2)}) async-start(), calls=%async_computation.20 | async-start | bytes 10485760 | tf_op jit(solution)/shard_map/psum | solution.py:269
  376.9 45.7 %copy-start.46 = (f32[320]{0:T(512)S(1)}, f32[320]{0:T(512)}, u32[]{:S(2)}) copy-start(f32[320]{0:T(512)} %param.25) | copy-start | bytes 3844
  376.9 45.7 %copy-start.49 = (f32[256,1]{0,1:T(1,128)S(1)}, f32[256,1]{0,1:T(1,128)}, u32[]{:S(2)}) copy-start(f32[256,1]{0,1:T(1,128)} %copy-done.48) | copy-start | bytes 3076
  377.0 45.7 %copy-start.3 = (f32[256,320]{0,1:T(8,128)S(1)}, f32[256,320]{0,1:T(8,128)}, u32[]{:S(2)}) copy-start(f32[256,320]{0,1:T(8,128)} %param.16) | copy-start | bytes 983044
  377.0 52.3 %copy-start.63 = (f32[256,1]{0,1:T(1,128)S(1)}, f32[256,1]{0,1:T(1,128)}, u32[]{:S(2)}) copy-start(f32[256,1]{0,1:T(1,128)} %get-tuple-element.90) | copy-start | bytes 3076
  377.0 54.1 %copy-start.59 = (f32[320]{0:T(512)S(1)}, f32[320]{0:T(512)}, u32[]{:S(2)}) copy-start(f32[320]{0:T(512)} %get-tuple-element.70) | copy-start | bytes 3844
  377.0 54.1 %copy-start.60 = (f32[320]{0:T(512)S(1)}, f32[320]{0:T(512)}, u32[]{:S(2)}) copy-start(f32[320]{0:T(512)} %get-tuple-element.72) | copy-start | bytes 3844
  377.0 54.1 %copy-start.61 = (f32[320]{0:T(512)S(1)}, f32[320]{0:T(512)}, u32[]{:S(2)}) copy-start(f32[320]{0:T(512)} %get-tuple-element.74) | copy-start | bytes 3844
  377.0 287.6 %all-reduce.11.cloned.1.call-start = ((), (), s32[]{:S(2)}) async-start(), calls=%async_computation.19 | async-start | bytes 1310720 | tf_op jit(solution)/shard_map/psum | solution.py:272
  573.3 96.7 %copy-start.32 = (f32[512,320]{0,1:T(8,128)S(1)}, f32[512,320]{0,1:T(8,128)}, u32[]{:S(2)}) copy-start(f32[512,320]{0,1:T(8,128)} %get-tuple-element.128) | copy-start | bytes 1966084
  573.3 97.6 %copy-start.28 = (f32[1024,320]{0,1:T(8,128)S(1)}, f32[1024,320]{0,1:T(8,128)}, u32[]{:S(2)}) copy-start(f32[1024,320]{0,1:T(8,128)} %get-tuple-element.131) | copy-start | bytes 3932164
  (49 other events, 448.1 us)
Sparse Core Ops, SparseCore 0:
  23.1 33.6 reduce-scatter.8
  73.1 8.0 reduce-scatter.10
  99.4 55.5 reduce-scatter.12
  157.9 21.2 all-gather.3
  181.9 8.0 reduce-scatter.14
  209.4 33.0 reduce-scatter.16
  245.8 33.0 all-gather.5
  282.3 8.0 reduce-scatter.18
  308.7 21.4 reduce-scatter.20
  346.1 21.2 all-gather.7
  370.2 8.0 reduce-scatter.22
  383.4 186.3 all-reduce.12
  573.8 90.7 all-reduce.10
where the time goes:
time: 680 us; the launch traced here: 678 us
  waiting for transfers between devices  436 us (64%)
  blocking collectives  135 us (20%)
  other arithmetic  32.6 us (5%)
  matrix products  29.4 us (4%)
  local copies, waits for them, and re-layouts  28.5 us (4%)
  between operations  15.3 us (2%)
    psum x1, waiting for transfers between devices, on_device(): lax.psum((query_part_grad, out_grad, mix_grad, down_grad), 'dp')  105 us
    psum x1, waiting for transfers between devices, on_device(): lax.psum((key_part_grad, value_part_grad, input_part, attn_part, pre_part...  91.3 us
    reduce_scatter x2, waiting for transfers between devices, project_sum(): lax.psum_scatter(rows_term(gathered, weight, contract), 'row', scatter_di...  64.9 us
    reduce_scatter x1, waiting for transfers between devices, on_device(): lax.psum_scatter(rows_term(ffn_all, mix_weight, 0), 'row', scatter_dimens...  55.6 us
    psum x1, blocking collectives, on_device(): lax.psum((query_gain_part, key_gain_part), ('dp', 'row', 'col'))  44.1 us
    all_gather x2, waiting for transfers between devices, hidden_gather(): return lax.all_gather(values, 'row', axis=0, tiled=True)  42.7 us
    psum x8, blocking collectives, width_total(): return lax.psum(values, 'row')  41 us
    psum x1, blocking collectives, on_device(): lax.psum((key_part_grad, value_part_grad, input_part, attn_part, pre_part...  33.6 us
  transfers between devices with their start and end apart: 13, of which 12 were waited for; matrix products, arithmetic and copies ran while one was open for 3% of the time, Pallas kernels for 0%

commit v1 on v0

--- a/solution.py
+++ b/solution.py
@@ -7,6 +7,20 @@
 HD = 256
 eps_norm = 1e-06
 rope_base = 1000000.0
+
+
+def files_measure(vec, shard_axis):
+    response = lax.axis_size(shard_axis)
+    state_next, everything = (response, lax.axis_index(shard_axis))
+    b_now, moved = (vec, 1)
+    while moved < state_next:
+        x_new = tuple(((dd, dd ^ moved) for dd in range(state_next)))
+        reply = lax.ppermute(b_now, shard_axis, x_new)
+        part_now = jnp.concatenate([b_now, reply], axis=0)
+        long_array = jnp.concatenate([reply, b_now], axis=0)
+        b_now = jnp.where(everything & moved == 0, part_now, long_array)
+        moved = 2 * moved
+    return b_now
 
 
 def rms_scale(values):
@@ -62,7 +76,7 @@
 
 
 def hidden_gather(values):
-    return lax.all_gather(values, "row", axis=0, tiled=True)
+    return files_measure(values, "row")
 
 
 def rows_term(gathered, weight, contract):

time: 680 us -> 659 us (0.969)
  waiting for transfers between devices: 436 us -> 419 us
    all_gather x2 -> x0, waiting for transfers between devices: 42.7 us -> none  [hidden_gather(): return lax.all_gather(values, 'row', axis=0, tiled=True)]
    ppermute x0 -> x2, waiting for transfers between devices: none -> 26.3 us  [files_measure(): reply = lax.ppermute(b_now, shard_axis, x_new)]
    unnamed x144 -> x164, local copies, waits for them, and re-layouts: 15.5 us -> 14.3 us
where the time goes in v1:
time: 659 us; the launch traced here: 658 us
  waiting for transfers between devices  419 us (64%)
  blocking collectives  135 us (20%)
  other arithmetic  32.1 us (5%)
  matrix products  28.7 us (4%)
  local copies, waits for them, and re-layouts  26.1 us (4%)
  between operations  15.5 us (2%)
    psum x1, waiting for transfers between devices, on_device(): lax.psum((query_part_grad, out_grad, mix_grad, down_grad), 'dp')  104 us
    psum x1, waiting for transfers between devices, on_device(): lax.psum((key_part_grad, value_part_grad, input_part, attn_part, pre_part...  91.3 us
    reduce_scatter x2, waiting for transfers between devices, project_sum(): lax.psum_scatter(rows_term(gathered, weight, contract), 'row', scatter_di...  64.9 us
    reduce_scatter x1, waiting for transfers between devices, on_device(): lax.psum_scatter(rows_term(ffn_all, mix_weight, 0), 'row', scatter_dimens...  55.6 us
    psum x1, blocking collectives, on_device(): lax.psum((query_gain_part, key_gain_part), ('dp', 'row', 'col'))  44.7 us
    psum x8, blocking collectives, width_total(): return lax.psum(values, 'row')  40.9 us
    all_gather x1, waiting for transfers between devices, on_device(): grad_mix_all = lax.all_gather(grad_mix, 'row', axis=0, tiled=True)  33.2 us
    psum x1, blocking collectives, on_device(): lax.psum((key_part_grad, value_part_grad, input_part, attn_part, pre_part...  32.4 us
  transfers between devices with their start and end apart: 13, of which 12 were waited for; matrix products, arithmetic and copies ran while one was open for 3% of the time, Pallas kernels for 0%

profile of v1, /device:TPU:0, one launch (start us, length us, event | category | flops | bytes accessed | tf_op | source)
XLA Modules:
  0.0 658.1 jit_solution(13466384445955721293)
XLA Ops:
  8.4 5.9 psum.140
  21.0 2.1 fusion.54
  25.1 31.8 %reduce-scatter.9.cloned.1.call-done = f32[256,1024]{1,0:T(8,128)} async-done(((f32[512,1024]{1,0:T(8,128)}), f32[256,1024]{1,0:T(8,128)}) %reduce-scatter.9.cloned.1.call-update) | async-done | bytes 1048592 | tf_op jit(solution)/shard_map/reduce_scatter | solution.py:89
  62.5 8.6 %all_gather.19 = bf16[512,512]{0,1:T(8,128)(2,1)S(1)} all-gather(bf16[256,512]{0,1:T(8,128)(2,1)S(1)} %bitcast.103), channel_id=1, replica_groups=mesh['dp'=8,'row'=2,'col'=2] {'row'}, dimensions={0}, use_global_device_ids=true | all-gather | bytes 786432 | tf_op jit(solution)/shard_map/all_gather | solution.py:229
  75.4 5.8 reduce-scatter.11.cloned.1.call-done
  82.3 4.9 psum.141
  88.9 4.9 psum.142
  97.3 3.2 fusion.55
  100.6 55.6 %reduce-scatter.13.cloned.1.call-done = f32[256,2048]{1,0:T(8,128)} async-done(((f32[512,2048]{1,0:T(8,128)}), f32[256,2048]{1,0:T(8,128)}) %reduce-scatter.13.cloned.1.call-update) | async-done | bytes 2097168 | tf_op jit(solution)/shard_map/reduce_scatter | solution.py:236
  158.5 13.2 %collective-permute-done = bf16[256,1024]{1,0:T(8,128)(2,1)S(1)} collective-permute-done((bf16[256,1024]{1,0:T(8,128)(2,1)S(1)}, bf16[256,1024]{1,0:T(8,128)(2,1)S(1)}, u32[]{:S(2)}, u32[]{:S(2)}) %collective-permute-start) | collective-permute-done | bytes 524320 | tf_op jit(solution)/shard_map/ppermute | solution.py:18
  173.2 8.1 %reduce-scatter.15.cloned.1.call-done = f32[256,320]{0,1:T(8,128)} async-done(((f32[512,320]{0,1:T(8,128)}), f32[256,320]{0,1:T(8,128)}) %reduce-scatter.15.cloned.1.call-update) | async-done | bytes 327696 | tf_op jit(solution)/shard_map/reduce_scatter | solution.py:95
  182.3 4.9 psum.143
  189.0 4.9 psum.144
  198.6 2.1 fusion.56
  200.7 33.2 %reduce-scatter.17.cloned.1.call-done = f32[256,1024]{1,0:T(8,128)} async-done(((f32[512,1024]{1,0:T(8,128)}), f32[256,1024]{1,0:T(8,128)}) %reduce-scatter.17.cloned.1.call-update) | async-done | bytes 1048592 | tf_op jit(solution)/shard_map/reduce_scatter | solution.py:89
  233.9 2.0 fusion.10
  237.1 33.2 %all-gather.2.cloned.1.call-done = bf16[512,2048]{1,0:T(8,128)(2,1)} async-done(((bf16[256,2048]{1,0:T(8,128)(2,1)}), bf16[512,2048]{1,0:T(8,128)(2,1)}) %all-gather.2.cloned.1.call-update) | async-done | bytes 2097168 | tf_op jit(solution)/shard_map/all_gather | solution.py:253
  270.2 3.3 fusion.57
  273.6 8.1 %reduce-scatter.19.cloned.1.call-done = f32[256,320]{0,1:T(8,128)} async-done(((f32[512,320]{0,1:T(8,128)}), f32[256,320]{0,1:T(8,128)}) %reduce-scatter.19.cloned.1.call-update) | async-done | bytes 327696 | tf_op jit(solution)/shard_map/reduce_scatter | solution.py:95
  283.5 4.9 psum.145
  290.3 5.0 psum.146
  298.2 2.5 fusion.58
  301.0 21.4 %reduce-scatter.21.cloned.1.call-done = f32[256,512]{1,0:T(8,128)} async-done(((f32[512,512]{1,0:T(8,128)}), f32[256,512]{1,0:T(8,128)}) %reduce-scatter.21.cloned.1.call-update) | async-done | bytes 524304 | tf_op jit(solution)/shard_map/reduce_scatter | solution.py:260
  334.8 13.2 %collective-permute-done.1 = bf16[256,1024]{1,0:T(8,128)(2,1)S(1)} collective-permute-done((bf16[256,1024]{1,0:T(8,128)(2,1)S(1)}, bf16[256,1024]{1,0:T(8,128)(2,1)S(1)}, u32[]{:S(2)}, u32[]{:S(2)}) %collective-permute-start.1) | collective-permute-done | bytes 524320 | tf_op jit(solution)/shard_map/ppermute | solution.py:18
  351.0 3.3 fusion.31
  354.3 2.4 fusion.62
  359.5 44.7 %all-reduce.4 = (f32[256]{0:T(256)}, f32[256]{0:T(256)}) all-reduce(f32[256]{0:T(256)S(1)} %get-tuple-element.68, f32[256]{0:T(256)S(1)} %get-tuple-element.56), channel_id=1, replica_groups=mesh['dp'=8,'row'=2,'col'=2] {'dp','row','col'}, use_global_device_ids=true, to_apply=%region_47.48 | all-reduce | flops 512 | bytes 4096 | tf_op jit(solution)/shard_map/psum | solution.py:289
  406.4 5.4 psum.147
  413.6 32.4 %all-reduce.5 = (f32[320]{0:T(512)}, f32[320]{0:T(512)}, f32[320]{0:T(512)}, f32[320]{0:T(512)}) all-reduce(f32[320]{0:T(512)S(1)} %get-tuple-element.76, f32[320]{0:T(512)S(1)} %copy-done.70, f32[320]{0:T(512)S(1)} %copy-done.69, f32[320]{0:T(512)S(1)} %copy-done.68), channel_id=1, replica_groups=mesh['dp'=8,'row'=2,'col'=2] {'dp','col'}, use_global_device_ids=true, to_apply=%region_39.40 | all-reduce | flops 1280 | bytes 10240 | tf_op jit(solution)/shard_map/psum | solution.py:286
  446.1 104.5 %all-reduce.13.cloned.1.call-done = (f32[320,512]{1,0:T(8,128)}, f32[512,320]{0,1:T(8,128)}, f32[320,2048]{1,0:T(8,128)}, f32[1024,320]{0,1:T(8,128)}) async-done(((f32[320,512]{1,0:T(8,128)}, f32[512,320]{0,1:T(8,128)}, f32[320,2048]{1,0:T(8,128)}, f32[1024,320]{0,1:T(8,128)}), (f32[320,512]{1,0:T(8,128)}, f32[512,320]{0,1:T(8,128)}, f32[320,2048]{1,0:T(8,128)}, ...) | async-done | bytes 5242896 | tf_op jit(solution)/shard_map/psum | solution.py:283
  550.6 3.6 fusion.52
  554.2 91.3 %all-reduce.11.cloned.1.call-done = (f32[320,256]{1,0:T(8,128)}, f32[320,256]{1,0:T(8,128)}) async-done(((f32[320,256]{1,0:T(8,128)}, f32[320,256]{1,0:T(8,128)}), (f32[320,256]{1,0:T(8,128)}, f32[320,256]{1,0:T(8,128)})) %all-reduce.11.cloned.1.call-update) | async-done | bytes 655376 | tf_op jit(solution)/shard_map/psum | solution.py:286
  (263 shorter events, 72.3 us)
Async XLA Ops:
  7.2 164.5 %copy-start = (bf16[1024,320]{0,1:T(8,128)(2,1)S(1)}, bf16[1024,320]{0,1:T(8,128)(2,1)}, u32[]{:S(2)}) copy-start(bf16[1024,320]{0,1:T(8,128)(2,1)} %param.24) | copy-start | bytes 1966084
  7.2 49.7 %reduce-scatter.9.cloned.1.call-start = ((), (), s32[]{:S(2)}) async-start(), calls=%async_computation.8 | async-start | bytes 3145728 | tf_op jit(solution)/shard_map/reduce_scatter | solution.py:89
  23.0 36.9 %copy-start.58 = (f32[256]{0:T(256)S(1)}, f32[256]{0:T(256)}, u32[]{:S(2)}) copy-start(f32[256]{0:T(256)} %param.30) | copy-start | bytes 3076
  23.1 58.2 %reduce-scatter.11.cloned.1.call-start = ((), (), s32[]{:S(2)}) async-start(), calls=%async_computation.9 | async-start | bytes 983040 | tf_op jit(solution)/shard_map/reduce_scatter | solution.py:95
  24.8 35.9 %copy-start.75 = (f32[128]{0:T(128)}, f32[128]{0:T(128)S(1)}, u32[]{:S(2)}) copy-start(f32[128]{0:T(128)S(1)} %negate_power_fusion) | copy-start | bytes 1540
  25.0 35.7 %copy-start.61 = (f32[256]{0:T(256)}, f32[256]{0:T(256)S(1)}, u32[]{:S(2)}) copy-start(f32[256]{0:T(256)S(1)} %fusion.43) | copy-start | bytes 3076
  73.1 83.2 %reduce-scatter.13.cloned.1.call-start = ((), (), s32[]{:S(2)}) async-start(), calls=%async_computation.10 | async-start | bytes 6291456 | tf_op jit(solution)/shard_map/reduce_scatter | solution.py:236
  88.9 105.1 %copy-start.4 = (f32[256,320]{0,1:T(8,128)}, f32[256,320]{0,1:T(8,128)S(1)}, u32[]{:S(2)}) copy-start(f32[256,320]{0,1:T(8,128)S(1)} %get-tuple-element.100) | copy-start | bytes 983044
  100.6 80.7 %reduce-scatter.15.cloned.1.call-start = ((), (), s32[]{:S(2)}) async-start(), calls=%async_computation.11 | async-start | bytes 983040 | tf_op jit(solution)/shard_map/reduce_scatter | solution.py:95
  158.1 13.6 %collective-permute-start = (bf16[256,1024]{1,0:T(8,128)(2,1)S(1)}, bf16[256,1024]{1,0:T(8,128)(2,1)S(1)}, u32[]{:S(2)}, u32[]{:S(2)}) collective-permute-start(bf16[256,1024]{1,0:T(8,128)(2,1)S(1)} %multiply_convert_fusion.1), channel_id=1, source_target_pairs={{0,2},{2,0},{1,3},{3,1},{4,6},{6,4},{5,7},{7,5},{8,10},{10,8},{9,1... | collective-permute-start | bytes 1572872 | tf_op jit(solution)/shard_map/ppermute | solution.py:18
  173.1 60.7 %reduce-scatter.17.cloned.1.call-start = ((), (), s32[]{:S(2)}) async-start(), calls=%async_computation.12 | async-start | bytes 3145728 | tf_op jit(solution)/shard_map/reduce_scatter | solution.py:89
  198.6 35.3 %copy-start.1 = (f32[256,2048]{1,0:T(8,128)S(1)}, f32[256,2048]{1,0:T(8,128)}, u32[]{:S(2)}) copy-start(f32[256,2048]{1,0:T(8,128)} %reduce-scatter.13.cloned.1.call-done) | copy-start | bytes 6291460
  200.6 69.6 %all-gather.2.cloned.1.call-start = ((), (), s32[]{:S(2)}) async-start(), calls=%async_computation.13 | async-start | bytes 3145728 | tf_op jit(solution)/shard_map/all_gather | solution.py:253
  237.0 44.8 %copy-start.5 = (f32[256,320]{0,1:T(8,128)S(1)}, f32[256,320]{0,1:T(8,128)}, u32[]{:S(2)}) copy-start(f32[256,320]{0,1:T(8,128)} %copy-done.4) | copy-start | bytes 983044
  237.0 51.4 %copy-start.6 = (f32[256,320]{0,1:T(8,128)S(1)}, f32[256,320]{0,1:T(8,128)}, u32[]{:S(2)}) copy-start(f32[256,320]{0,1:T(8,128)} %reduce-scatter.11.cloned.1.call-done) | copy-start | bytes 983044
  237.0 51.4 %copy-start.16 = (f32[256,320]{0,1:T(8,128)S(1)}, f32[256,320]{0,1:T(8,128)}, u32[]{:S(2)}) copy-start(f32[256,320]{0,1:T(8,128)} %param.31) | copy-start | bytes 983044
  237.0 44.7 %reduce-scatter.19.cloned.1.call-start = ((), (), s32[]{:S(2)}) async-start(), calls=%async_computation.14 | async-start | bytes 983040 | tf_op jit(solution)/shard_map/reduce_scatter | solution.py:95
  273.6 48.8 %reduce-scatter.21.cloned.1.call-start = ((), (), s32[]{:S(2)}) async-start(), calls=%async_computation.15 | async-start | bytes 1572864 | tf_op jit(solution)/shard_map/reduce_scatter | solution.py:260
  300.7 104.4 %reduce-scatter.23.cloned.1.call-start = ((), (), s32[]{:S(2)}) async-start(), calls=%async_computation.16 | async-start | bytes 983040 | tf_op jit(solution)/shard_map/reduce_scatter | solution.py:95
  334.4 13.6 %collective-permute-start.1 = (bf16[256,1024]{1,0:T(8,128)(2,1)S(1)}, bf16[256,1024]{1,0:T(8,128)(2,1)S(1)}, u32[]{:S(2)}, u32[]{:S(2)}) collective-permute-start(bf16[256,1024]{1,0:T(8,128)(2,1)S(1)} %pad_maximum_fusion.1), channel_id=1, source_target_pairs={{0,2},{2,0},{1,3},{3,1},{4,6},{6,4},{5,7},{7,5},{8,10},{10,8},{9,1... | collective-permute-start | bytes 1572872 | tf_op jit(solution)/shard_map/ppermute | solution.py:18
  351.0 199.6 %all-reduce.13.cloned.1.call-start = ((), (), s32[]{:S(2)}) async-start(), calls=%async_computation.18 | async-start | bytes 10485760 | tf_op jit(solution)/shard_map/psum | solution.py:283
  359.3 45.8 %copy-start.49 = (f32[320]{0:T(512)S(1)}, f32[320]{0:T(512)}, u32[]{:S(2)}) copy-start(f32[320]{0:T(512)} %param.25) | copy-start | bytes 3844
  359.3 45.8 %copy-start.54 = (f32[256,1]{0,1:T(1,128)S(1)}, f32[256,1]{0,1:T(1,128)}, u32[]{:S(2)}) copy-start(f32[256,1]{0,1:T(1,128)} %copy-done.53) | copy-start | bytes 3076
  359.4 45.8 %copy-start.3 = (f32[256,320]{0,1:T(8,128)S(1)}, f32[256,320]{0,1:T(8,128)}, u32[]{:S(2)}) copy-start(f32[256,320]{0,1:T(8,128)} %param.16) | copy-start | bytes 983044
  359.4 52.4 %copy-start.72 = (f32[256,1]{0,1:T(1,128)S(1)}, f32[256,1]{0,1:T(1,128)}, u32[]{:S(2)}) copy-start(f32[256,1]{0,1:T(1,128)} %get-tuple-element.90) | copy-start | bytes 3076
  359.4 54.2 %copy-start.68 = (f32[320]{0:T(512)S(1)}, f32[320]{0:T(512)}, u32[]{:S(2)}) copy-start(f32[320]{0:T(512)} %get-tuple-element.70) | copy-start | bytes 3844
  359.4 54.2 %copy-start.69 = (f32[320]{0:T(512)S(1)}, f32[320]{0:T(512)}, u32[]{:S(2)}) copy-start(f32[320]{0:T(512)} %get-tuple-element.72) | copy-start | bytes 3844
  359.4 54.2 %copy-start.70 = (f32[320]{0:T(512)S(1)}, f32[320]{0:T(512)}, u32[]{:S(2)}) copy-start(f32[320]{0:T(512)} %get-tuple-element.74) | copy-start | bytes 3844
  359.4 286.0 %all-reduce.11.cloned.1.call-start = ((), (), s32[]{:S(2)}) async-start(), calls=%async_computation.17 | async-start | bytes 1310720 | tf_op jit(solution)/shard_map/psum | solution.py:286
  550.6 94.9 %copy-start.36 = (f32[320,512]{1,0:T(8,128)S(1)}, f32[320,512]{1,0:T(8,128)}, u32[]{:S(2)}) copy-start(f32[320,512]{1,0:T(8,128)} %get-tuple-element.125) | copy-start | bytes 1966084
  554.1 95.5 %copy-start.35 = (f32[512,320]{0,1:T(8,128)S(1)}, f32[512,320]{0,1:T(8,128)}, u32[]{:S(2)}) copy-start(f32[512,320]{0,1:T(8,128)} %get-tuple-element.128) | copy-start | bytes 1966084
  554.2 96.4 %copy-start.27 = (f32[1024,320]{0,1:T(8,128)S(1)}, f32[1024,320]{0,1:T(8,128)}, u32[]{:S(2)}) copy-start(f32[1024,320]{0,1:T(8,128)} %get-tuple-element.131) | copy-start | bytes 3932164
  (59 other events, 448.2 us)
Sparse Core Ops, SparseCore 0:
  23.2 33.6 reduce-scatter.8
  73.2 8.0 reduce-scatter.10
  100.7 55.4 reduce-scatter.12
  173.2 8.0 reduce-scatter.14
  200.8 33.0 reduce-scatter.16
  237.1 33.0 all-gather.1
  273.7 8.0 reduce-scatter.18
  300.8 21.4 reduce-scatter.20
  351.1 8.0 reduce-scatter.22
  364.2 186.2 all-reduce.12
  554.6 90.7 all-reduce.10
